TPU v7x, 512 devices: a whole 4x4x16 slice. The times are simulated.
512 devices in a mesh: grp: 16 (over z), shard: 32 (over y, x, core).
Axes of the slice: x: 4, y: 4, z: 16, core: 2. Of those that a mesh axis runs over, the one named last changes fastest.
Arguments:
- activations: bfloat16 [1024, 5120], P('grp', 'shard'), may hold values from -6 to 6
- grad_outputs: bfloat16 [1024, 27648], P('shard', 'grp'), may hold values from -6 to 6
- basis_in: bfloat16 [5120, 2560], P('shard', 'grp'), may hold values from -0.078125 to 0.078125
- basis_out: bfloat16 [27648, 13824], P('grp', 'shard'), may hold values from -0.0390625 to 0.0390625
- query_grads: bfloat16 [16, 2560, 13824], P('grp', None, 'shard'), may hold values from -0.0009765625 to 0.0009765625
Outputs:
- scores: float32 [16, 1024], P('grp', 'shard')
All inputs are finite; a program needn't handle non-finite values.
Results may differ from a plain program's by a relative error of at most 0.0041.
Values may be sent and summed in bfloat16 or wider, within the bound.
No kernel may reach another device: no remote copies, remote signals or barrier semaphores. Data moves between devices by JAX's collectives and lax.ppermute only.
A program may use at most 64 MiB of HBM per device.

v0:
```python
import jax
import jax.numpy as jnp
from jax import lax
from jax.sharding import PartitionSpec as P


def local(activations, grad_outputs, basis_in, basis_out, query_grads):
    full_in = lax.all_gather(basis_in, "grp", axis=1, tiled=True)
    act_terms = lax.dot_general(
        full_in, activations, (((0,), (1,)), ((), ())), preferred_element_type=jnp.float32
    )
    act_local = lax.psum(act_terms, "shard").astype(jnp.bfloat16)
    act_rot = lax.all_gather(act_local, "grp", axis=1, tiled=True)
    out_terms = jnp.dot(
        lax.all_gather(grad_outputs, "shard", axis=0, tiled=True),
        basis_out,
        preferred_element_type=jnp.float32,
    )
    out_rot = lax.psum(out_terms, "grp").astype(jnp.bfloat16)
    mixed = lax.dot_general(
        act_rot, query_grads[0], (((0,), (0,)), ((), ())), preferred_element_type=jnp.float32
    )
    partial_scores = jnp.sum(mixed * out_rot.astype(jnp.float32), axis=1)
    return lax.psum_scatter(partial_scores[None, :], "shard", scatter_dimension=1, tiled=True)


def solution(mesh):
    placed = (
        P("grp", "shard"),
        P("shard", "grp"),
        P("shard", "grp"),
        P("grp", "shard"),
        P("grp", None, "shard"),
    )
    return jax.shard_map(
        local, mesh=mesh, in_specs=placed, out_specs=P("grp", "shard"), check_vma=False
    )
```

profile of v0, /device:TPU:2, one launch (start us, length us, event | category | flops | bytes accessed | tf_op | source)
XLA Modules:
  0.0 392.9 jit_solution(17154068372020771227)
XLA Ops:
  6.5 0.0 copy-start
  6.5 0.0 all-gather.5.cloned.1.call-start
  6.5 0.7 all-gather.5.cloned.1.call-update
  7.3 0.0 all-gather.3.cloned.1.call-start
  7.3 1.0 copy.6
  8.3 43.3 %all_gather.9 = bf16[160,2560]{0,1:T(8,128)(2,1)S(1)} all-gather(bf16[160,160]{0,1:T(8,128)(2,1)S(1)} %copy.6), channel_id=1, replica_groups=mesh['grp'=16,'shard'=32] {'grp'}, dimensions={1}, use_global_device_ids=true | all-gather | bytes 870400 | tf_op jit(solution)/shard_map/all_gather | solution.py:8
  51.6 1.3 fusion.4
  52.9 126.1 %all-reduce.3 = bf16[2560,64]{0,1:T(8,128)(2,1)} all-reduce(f32[2560,64]{0,1:T(8,128)S(1)} %fusion.4), channel_id=1, replica_groups=mesh['grp'=16,'shard'=32] {'shard'}, use_global_device_ids=true, to_apply=%region_0.0 | all-reduce | flops 163840 | bytes 983040 | tf_op jit(solution)/shard_map/psum | solution.py:12
  178.9 0.0 all-gather.3.cloned.1.call-update
  179.0 0.0 reduce-scatter.4.cloned.1.call-start
  179.0 0.0 all-gather.5.cloned.1.call-done
  179.0 5.5 %fusion.5 = f32[1024,432]{0,1:T(8,128)} fusion(bf16[1024,1728]{1,0:T(8,128)(2,1)} %all-gather.5.cloned.1.call-done, bf16[1728,432]{0,1:T(8,128)(2,1)} %param.8), kind=kOutput, calls=%fused_computation.4 | convolution fusion | flops 1528823808 | bytes 6801408 | tf_op jit(solution)/shard_map/dot_general | solution.py:14
  184.6 91.9 %all-reduce.2 = bf16[1024,432]{0,1:T(8,128)(2,1)S(1)} all-reduce(f32[1024,432]{0,1:T(8,128)} %fusion.5), channel_id=1, replica_groups=mesh['grp'=16,'shard'=32] {'grp'}, use_global_device_ids=true, to_apply=%region_1.0 | all-reduce | flops 442368 | bytes 2654208 | tf_op jit(solution)/shard_map/psum | solution.py:19
  276.4 4.1 %all-gather.3.cloned.1.call-done = bf16[2560,1024]{0,1:T(8,128)(2,1)} async-done(((bf16[2560,64]{0,1:T(8,128)(2,1)}), bf16[2560,1024]{0,1:T(8,128)(2,1)}) %all-gather.3.cloned.1.call-update) | async-done | bytes 5242896 | tf_op jit(solution)/shard_map/all_gather | solution.py:13
  280.5 0.0 copy-done
  280.5 5.0 %multiply_reduce_fusion = f32[1024]{0:T(1024)S(1)} fusion(bf16[2560,1024]{0,1:T(8,128)(2,1)} %all-gather.3.cloned.1.call-done, bf16[1,2560,432]{1,2,0:T(8,128)(2,1)S(1)} %copy-done, bf16[1024,432]{0,1:T(8,128)(2,1)S(1)} %all-reduce.2), kind=kOutput, calls=%fused_computation.2 | convolution fusion | flops 2266250240 | bytes 8343552 | tf_op jit(solution)/shard_map/dot_general | solution.py:20
  285.5 1.0 copy.7
  286.5 0.0 reduce-scatter.4.cloned.1.call-update
  286.5 98.5 %reduce-scatter.4.cloned.1.call-done = f32[32,1]{1,0:T(8,128)} async-done(((f32[1024,1]{1,0:T(8,128)}), f32[32,1]{1,0:T(8,128)}) %reduce-scatter.4.cloned.1.call-update) | async-done | bytes 144
  385.1 1.3 copy.8
Async XLA Ops:
  6.5 274.0 %copy-start = (bf16[1,2560,432]{1,2,0:T(8,128)(2,1)S(1)}, bf16[1,2560,432]{1,2,0:T(8,128)(2,1)}, u32[]{:S(2)}) copy-start(bf16[1,2560,432]{1,2,0:T(8,128)(2,1)} %param.9) | copy-start | bytes 6635524
  6.5 172.5 %all-gather.5.cloned.1.call-start = ((), (), s32[]{:S(2)}) async-start(), calls=%async_computation.2 | async-start | bytes 3784704 | tf_op jit(solution)/shard_map/all_gather | solution.py:15
  7.3 273.3 %all-gather.3.cloned.1.call-start = ((), (), s32[]{:S(2)}) async-start(), calls=%async_computation.1 | async-start | bytes 5570560 | tf_op jit(solution)/shard_map/all_gather | solution.py:13
  179.0 206.1 %reduce-scatter.4.cloned.1.call-start = ((), (), s32[]{:S(2)}) async-start(), calls=%async_computation.3 | async-start | bytes 540672
Sparse Core Ops, SparseCore 0:
  10.5 64.9 all-gather.4
  179.1 101.3 all-gather.2
  286.7 98.3 reduce-scatter.3
where the time goes:
time: 393 us
  blocking collectives  261 us (66%)
  waiting for transfers between devices  103 us (26%)
  between operations  13.1 us (3%)
  matrix products  11.8 us (3%)
    psum x1, blocking collectives, local(): act_local = lax.psum(act_terms, 'shard').astype(jnp.bfloat16)  126 us
    unnamed x4, waiting for transfers between devices  99.3 us
    psum x1, blocking collectives, local(): out_rot = lax.psum(out_terms, 'grp').astype(jnp.bfloat16)  91.9 us
    all_gather x1, blocking collectives, local(): full_in = lax.all_gather(basis_in, 'grp', axis=1, tiled=True)  43.3 us
  transfers between devices with their start and end apart: 3, of which 2 were waited for; matrix products, arithmetic and copies ran while one was open for 2% of the time, Pallas kernels for 0%

commit v1 on v0

--- a/solution.py
+++ b/solution.py
@@ -5,7 +5,10 @@
 
 
 def local(activations, grad_outputs, basis_in, basis_out, query_grads):
-    full_in = lax.all_gather(basis_in, "grp", axis=1, tiled=True)
+    n_dev = lax.axis_size("grp")
+    shards = jnp.stack([basis_in for _ in range(n_dev)])
+    shards = lax.all_to_all(shards, "grp", split_axis=0, concat_axis=0)
+    full_in = jnp.concatenate(shards, axis=1)
     act_terms = lax.dot_general(
         full_in, activations, (((0,), (1,)), ((), ())), preferred_element_type=jnp.float32
     )

time: 393 us -> 435 us (1.11)
  blocking collectives: 261 us -> 301 us
    all_to_all x0 -> x1, blocking collectives: none -> 78.7 us  [local(): shards = lax.all_to_all(shards, 'grp', split_axis=0, concat_axis=0)]
    all_gather x1 -> x0, blocking collectives: 43.3 us -> none  [local(): full_in = lax.all_gather(basis_in, 'grp', axis=1, tiled=True)]
    psum x1, blocking collectives: 91.9 us -> 97.2 us  [local(): out_rot = lax.psum(out_terms, 'grp').astype(jnp.bfloat16)]
  transfers between devices with their start and end apart: 3 -> 3, of which waited for: 2 -> 2; matrix products, arithmetic and copies ran while one was open for 2% -> 3% of each run, Pallas kernels for 0% -> 0%
where the time goes in v1:
time: 435 us
  blocking collectives  301 us (69%)
  waiting for transfers between devices  102 us (23%)
  between operations  13.2 us (3%)
  matrix products  11.9 us (3%)
  local copies, waits for them, and re-layouts  6.79 us (2%)
    psum x1, blocking collectives, local(): act_local = lax.psum(act_terms, 'shard').astype(jnp.bfloat16)  125 us
    unnamed x4, waiting for transfers between devices  99.5 us
    psum x1, blocking collectives, local(): out_rot = lax.psum(out_terms, 'grp').astype(jnp.bfloat16)  97.2 us
    all_to_all x1, blocking collectives, local(): shards = lax.all_to_all(shards, 'grp', split_axis=0, concat_axis=0)  78.7 us
  transfers between devices with their start and end apart: 3, of which 2 were waited for; matrix products, arithmetic and copies ran while one was open for 3% of the time, Pallas kernels for 0%

profile of v1, /device:TPU:2, one launch (start us, length us, event | category | flops | bytes accessed | tf_op | source)
XLA Modules:
  0.0 435.0 jit_solution(5549883376780402374)
XLA Ops:
  6.5 0.0 copy-start
  6.5 0.0 all-gather.5.cloned.1.call-start
  6.5 0.7 all-gather.5.cloned.1.call-update
  7.3 0.0 all-gather.3.cloned.1.call-start
  7.3 1.0 stack.2
  8.3 78.7 %all_to_all.5 = bf16[16,160,160]{2,1,0:T(8,128)(2,1)S(1)} all-to-all(bf16[16,160,160]{2,1,0:T(8,128)(2,1)S(1)} %stack.2), channel_id=1, replica_groups=mesh['grp'=16,'shard'=32] {'grp'}, dimensions={0} | all-to-all | bytes 1638400 | tf_op jit(solution)/shard_map/all_to_all | solution.py:10
  87.0 0.0 copy-start.1
  87.0 0.7 copy.6
  87.7 2.7 reshape.9
  90.5 0.0 copy-done.1
  90.5 1.4 fusion.5
  91.9 125.2 %all-reduce.3 = bf16[2560,64]{0,1:T(8,128)(2,1)} all-reduce(f32[2560,64]{0,1:T(8,128)S(1)} %fusion.5), channel_id=1, replica_groups=mesh['grp'=16,'shard'=32] {'shard'}, use_global_device_ids=true, to_apply=%region_0.0 | all-reduce | flops 163840 | bytes 983040 | tf_op jit(solution)/shard_map/psum | solution.py:15
  217.1 0.0 all-gather.3.cloned.1.call-update
  217.1 0.0 reduce-scatter.4.cloned.1.call-start
  217.2 0.0 all-gather.5.cloned.1.call-done
  217.2 5.5 %fusion.4 = f32[1024,432]{0,1:T(8,128)} fusion(bf16[1024,1728]{1,0:T(8,128)(2,1)} %all-gather.5.cloned.1.call-done, bf16[1728,432]{0,1:T(8,128)(2,1)} %param.8), kind=kOutput, calls=%fused_computation.3 | convolution fusion | flops 1528823808 | bytes 6801408 | tf_op jit(solution)/shard_map/dot_general | solution.py:17
  222.7 97.2 %all-reduce.2 = bf16[1024,432]{0,1:T(8,128)(2,1)S(1)} all-reduce(f32[1024,432]{0,1:T(8,128)} %fusion.4), channel_id=1, replica_groups=mesh['grp'=16,'shard'=32] {'grp'}, use_global_device_ids=true, to_apply=%region_1.0 | all-reduce | flops 442368 | bytes 2654208 | tf_op jit(solution)/shard_map/psum | solution.py:22
  320.0 2.5 all-gather.3.cloned.1.call-done
  322.4 0.0 copy-done
  322.4 5.0 %multiply_reduce_fusion = f32[1024]{0:T(1024)S(1)} fusion(bf16[2560,1024]{0,1:T(8,128)(2,1)} %all-gather.3.cloned.1.call-done, bf16[1,2560,432]{1,2,0:T(8,128)(2,1)S(1)} %copy-done, bf16[1024,432]{0,1:T(8,128)(2,1)S(1)} %all-reduce.2), kind=kOutput, calls=%fused_computation.2 | convolution fusion | flops 2266250240 | bytes 8343552 | tf_op jit(solution)/shard_map/dot_general | solution.py:23
  327.4 1.0 copy.7
  328.4 0.0 reduce-scatter.4.cloned.1.call-update
  328.5 98.7 %reduce-scatter.4.cloned.1.call-done = f32[32,1]{1,0:T(8,128)} async-done(((f32[1024,1]{1,0:T(8,128)}), f32[32,1]{1,0:T(8,128)}) %reduce-scatter.4.cloned.1.call-update) | async-done | bytes 144
  427.2 1.3 copy.8
Async XLA Ops:
  6.5 315.9 %copy-start = (bf16[1,2560,432]{1,2,0:T(8,128)(2,1)S(1)}, bf16[1,2560,432]{1,2,0:T(8,128)(2,1)}, u32[]{:S(2)}) copy-start(bf16[1,2560,432]{1,2,0:T(8,128)(2,1)} %param.9) | copy-start | bytes 6635524
  6.5 210.7 %all-gather.5.cloned.1.call-start = ((), (), s32[]{:S(2)}) async-start(), calls=%async_computation.3 | async-start | bytes 3784704 | tf_op jit(solution)/shard_map/all_gather | solution.py:18
  7.3 315.2 %all-gather.3.cloned.1.call-start = ((), (), s32[]{:S(2)}) async-start(), calls=%async_computation.2 | async-start | bytes 5570560 | tf_op jit(solution)/shard_map/all_gather | solution.py:16
  87.0 3.5 copy-start.1
  217.1 210.1 %reduce-scatter.4.cloned.1.call-start = ((), (), s32[]{:S(2)}) async-start(), calls=%async_computation.4 | async-start | bytes 540672
Sparse Core Ops, SparseCore 0:
  10.5 64.9 all-gather.4
  217.2 105.1 all-gather.2
  328.6 98.5 reduce-scatter.3

commit v2 on v0

--- a/solution.py
+++ b/solution.py
@@ -2,6 +2,11 @@
 import jax.numpy as jnp
 from jax import lax
 from jax.sharding import PartitionSpec as P
+
+
+def add_all(x, axis):
+    parts = lax.all_gather(x, axis)
+    return jnp.sum(parts, axis=0)
 
 
 def local(activations, grad_outputs, basis_in, basis_out, query_grads):
@@ -16,7 +21,7 @@
         basis_out,
         preferred_element_type=jnp.float32,
     )
-    out_rot = lax.psum(out_terms, "grp").astype(jnp.bfloat16)
+    out_rot = add_all(out_terms, "grp").astype(jnp.bfloat16)
     mixed = lax.dot_general(
         act_rot, query_grads[0], (((0,), (0,)), ((), ())), preferred_element_type=jnp.float32
     )

time: 393 us -> 584 us (1.49)
  waiting for transfers between devices: 103 us -> 352 us
  blocking collectives: 261 us -> 174 us
  local copies, waits for them, and re-layouts: 3.31 us -> 28.9 us
    all_gather x0 -> x1, waiting for transfers between devices: none -> 139 us  [add_all(): parts = lax.all_gather(x, axis)]
    psum x1 -> x0, blocking collectives: 91.9 us -> none  [local(): out_rot = lax.psum(out_terms, 'grp').astype(jnp.bfloat16)]
    all_gather x1, waiting for transfers between devices: 0.02 us -> 68.1 us  [local(): lax.all_gather(grad_outputs, 'shard', axis=0, tiled=True)]
    all_gather x1, waiting for transfers between devices: 4.07 us -> 47.2 us  [local(): act_rot = lax.all_gather(act_local, 'grp', axis=1, tiled=True)]
    unnamed x5 -> x10, local copies, waits for them, and re-layouts: 3.31 us -> 28.9 us
    unnamed x4 -> x5, waiting for transfers between devices: 99.3 us -> 97.3 us
  transfers between devices with their start and end apart: 3 -> 4, of which waited for: 2 -> 4; matrix products, arithmetic and copies ran while one was open for 2% -> 6% of each run, Pallas kernels for 0% -> 0%
where the time goes in v2:
time: 584 us
  waiting for transfers between devices  352 us (60%)
  blocking collectives  174 us (30%)
  local copies, waits for them, and re-layouts  28.9 us (5%)
  between operations  13.2 us (2%)
  matrix products  11 us (2%)
    all_gather x1, waiting for transfers between devices, add_all(): parts = lax.all_gather(x, axis)  139 us
    psum x1, blocking collectives, local(): act_local = lax.psum(act_terms, 'shard').astype(jnp.bfloat16)  125 us
    unnamed x5, waiting for transfers between devices  97.3 us
    all_gather x1, waiting for transfers between devices, local(): lax.all_gather(grad_outputs, 'shard', axis=0, tiled=True)  68.1 us
    all_gather x1, blocking collectives, local(): full_in = lax.all_gather(basis_in, 'grp', axis=1, tiled=True)  48.6 us
    all_gather x1, waiting for transfers between devices, local(): act_rot = lax.all_gather(act_local, 'grp', axis=1, tiled=True)  47.2 us
    unnamed x10, local copies, waits for them, and re-layouts  28.9 us
  transfers between devices with their start and end apart: 4, of which 4 were waited for; matrix products, arithmetic and copies ran while one was open for 6% of the time, Pallas kernels for 0%

profile of v2, /device:TPU:2, one launch (start us, length us, event | category | flops | bytes accessed | tf_op | source)
XLA Modules:
  0.0 584.2 jit_solution(3614422358583993850)
XLA Ops:
  6.5 0.0 copy-start
  6.5 0.0 all-gather.7.cloned.1.call-start
  6.5 0.7 all-gather.7.cloned.1.call-update
  7.3 0.0 all-gather.9.cloned.1.call-start
  7.3 68.1 %all-gather.7.cloned.1.call-done = bf16[1024,1728]{1,0:T(8,128)(2,1)} async-done(((bf16[32,1728]{1,0:T(8,128)(2,1)}), bf16[1024,1728]{1,0:T(8,128)(2,1)}) %all-gather.7.cloned.1.call-update) | async-done | bytes 3538960 | tf_op jit(solution)/shard_map/all_gather | solution.py:20
  75.5 5.5 fusion.5
  81.0 0.0 all-gather.9.cloned.1.call-update
  81.0 0.0 all-gather.5.cloned.1.call-start
  81.0 0.1 copy.6
  81.1 48.6 %all_gather.15 = bf16[160,2560]{0,1:T(8,128)(2,1)S(1)} all-gather(bf16[160,160]{0,1:T(8,128)(2,1)S(1)} %copy.6), channel_id=1, replica_groups=mesh['grp'=16,'shard'=32] {'grp'}, dimensions={1}, use_global_device_ids=true | all-gather | bytes 870400 | tf_op jit(solution)/shard_map/all_gather | solution.py:13
  129.7 0.5 fusion.4
  130.2 125.4 %all-reduce.1 = bf16[2560,64]{0,1:T(8,128)(2,1)} all-reduce(f32[2560,64]{0,1:T(8,128)S(1)} %fusion.4), channel_id=1, replica_groups=mesh['grp'=16,'shard'=32] {'shard'}, use_global_device_ids=true, to_apply=%region_0.0 | all-reduce | flops 163840 | bytes 983040 | tf_op jit(solution)/shard_map/psum | solution.py:17
  255.7 0.0 all-gather.5.cloned.1.call-update
  255.7 0.0 reduce-scatter.4.cloned.1.call-start
  255.7 138.9 %all-gather.9.cloned.1.call-done = f32[16384,432]{0,1:T(8,128)} async-done(((f32[1024,432]{0,1:T(8,128)}), f32[16384,432]{0,1:T(8,128)}) %all-gather.9.cloned.1.call-update) | async-done | bytes 28311568 | tf_op jit(solution)/shard_map/all_gather | solution.py:8
  394.7 26.4 %copy.9 = f32[54,8,16,1024]{3,2,1,0:T(8,128)S(1)} copy(f32[54,8,16,1024]{3,1,2,0:T(8,128)} %bitcast.18) | data formatting | bytes 56623104
  421.1 5.4 bitcast_reduce_fusion
  426.5 47.2 %all-gather.5.cloned.1.call-done = bf16[2560,1024]{0,1:T(8,128)(2,1)} async-done(((bf16[2560,64]{0,1:T(8,128)(2,1)}), bf16[2560,1024]{0,1:T(8,128)(2,1)}) %all-gather.5.cloned.1.call-update) | async-done | bytes 5242896 | tf_op jit(solution)/shard_map/all_gather | solution.py:18
  473.8 0.0 copy-done
  473.8 5.0 multiply_reduce_fusion
  478.7 1.0 copy.7
  479.8 0.0 reduce-scatter.4.cloned.1.call-update
  479.8 96.6 %reduce-scatter.4.cloned.1.call-done = f32[32,1]{1,0:T(8,128)} async-done(((f32[1024,1]{1,0:T(8,128)}), f32[32,1]{1,0:T(8,128)}) %reduce-scatter.4.cloned.1.call-update) | async-done | bytes 144
  576.4 1.3 copy.8
  (4 shorter events, 0.0 us)
Async XLA Ops:
  6.5 467.2 %copy-start = (bf16[1,2560,432]{1,2,0:T(8,128)(2,1)S(1)}, bf16[1,2560,432]{1,2,0:T(8,128)(2,1)}, u32[]{:S(2)}) copy-start(bf16[1,2560,432]{1,2,0:T(8,128)(2,1)} %param.9) | copy-start | bytes 6635524
  6.5 68.9 %all-gather.7.cloned.1.call-start = ((), (), s32[]{:S(2)}) async-start(), calls=%async_computation.2 | async-start | bytes 3784704 | tf_op jit(solution)/shard_map/all_gather | solution.py:20
  7.3 73.8 %copy-start.1 = (bf16[160,160]{1,0:T(8,128)(2,1)S(1)}, bf16[160,160]{1,0:T(8,128)(2,1)}, u32[]{:S(2)}) copy-start(bf16[160,160]{1,0:T(8,128)(2,1)} %param.7) | copy-start | bytes 153604
  7.3 387.4 %all-gather.9.cloned.1.call-start = ((), (), s32[]{:S(2)}) async-start(), calls=%async_computation.3 | async-start | bytes 30081024 | tf_op jit(solution)/shard_map/all_gather | solution.py:8
  81.0 48.8 %copy-start.2 = (bf16[64,160]{1,0:T(8,128)(2,1)S(1)}, bf16[64,160]{1,0:T(8,128)(2,1)}, u32[]{:S(2)}) copy-start(bf16[64,160]{1,0:T(8,128)(2,1)} %param.5) | copy-start | bytes 61444
  81.0 392.8 %all-gather.5.cloned.1.call-start = ((), (), s32[]{:S(2)}) async-start(), calls=%async_computation.1 | async-start | bytes 5570560 | tf_op jit(solution)/shard_map/all_gather | solution.py:18
  255.7 320.7 %reduce-scatter.4.cloned.1.call-start = ((), (), s32[]{:S(2)}) async-start(), calls=%async_computation.4 | async-start | bytes 540672
Sparse Core Ops, SparseCore 0:
  10.5 64.9 all-gather.6
  81.1 313.5 all-gather.8
  396.8 76.9 all-gather.4
  479.9 96.4 reduce-scatter.3
